TPU v7x, 512 devices: a whole 4x8x8 slice. The times are simulated.
512 devices in a mesh: req: 64 (over x, y, core), tp: 8 (over z).
Axes of the slice: x: 4, y: 8, z: 8, core: 2. Of those that a mesh axis runs over, the one named last changes fastest.
Arguments:
- queries: bfloat16 [64, 28, 4096], P('req', None, 'tp'), may hold values from -25 to 25
- tree_kv: bfloat16 [64, 28, 2048], P('req', None, 'tp'), may hold values from -4 to 4
- tree_parent: int32 [64, 28], P('req'), may hold values from -1 to 26, as said below
- accepted_path: int32 [64, 8], replicated, may hold values from -1 to 27, as said below
- cache_kv: bfloat16 [192, 256, 2048], P('req', None, 'tp'), may hold values from -6 to 6
- piece_owner: int32 [192, 2], P('req'), may hold values from -1 to 63, as said below
- cache_len: int32 [64], replicated, may hold values from 1 to 1016, as said below
- out_weight: bfloat16 [4096, 4096], P('tp', 'req'), may hold values from -0.09375 to 0.09375
Outputs:
- mixed: bfloat16 [64, 28, 4096], P('tp', None, 'req')
- cache_out: bfloat16 [192, 256, 2048], P('req', None, 'tp')
Inputs may be any that keep to these rules, and one draw needn't show every extreme that they name: tree_parent[r, 0] = -1 and 0 <= tree_parent[r, i] < i for i >= 1; tokens 1 to 7 have parent i - 1. accepted_path[r] lists, root first, the tokens on the path from token 0 to some token of request r's tree, then -1 entries; it holds 1 to 8 tokens, and 8 for some request. piece_owner[s] = (r, p) means slot s holds cache rows p * 256 to p * 256 + 255 of request r; (-1, -1) marks an unused slot. For each request r the pieces 0 to (cache_len[r] + 7) // 256 stand in exactly one slot each, and no other pieces do. cache_len[r] + 8 <= 1024.
All inputs are finite; a program needn't handle non-finite values.
Results may differ from a plain program's by a relative error of at most 0.02.
Values may be sent and summed in bfloat16 or wider, within the bound.
No kernel may reach another device: no remote copies, remote signals or barrier semaphores. Data moves between devices by JAX's collectives and lax.ppermute only.
A program may use at most 64 MiB of HBM per device.

v0:
```python
import math
import jax
import jax.numpy as jnp
from jax import lax
from jax.sharding import PartitionSpec as P

HD = 128
NEG = -1e30


def ancestors(parent):
    tree_size = parent.shape[-1]
    node_ids = lax.broadcasted_iota(jnp.int32, (tree_size, tree_size), 1)
    parent_hot = (parent[..., :, None] == node_ids).astype(jnp.float32)
    reached = jnp.minimum(parent_hot + jnp.eye(tree_size, dtype=jnp.float32), 1.0)
    for rounds in range(max(1, (tree_size - 1).bit_length())):
        reached = jnp.minimum(
            jnp.einsum("rij,rjk->rik", reached, reached, precision=lax.Precision.HIGHEST), 1.0
        )
    return reached


def shards(
    queries, tree_kv, tree_parent, accepted_path, cache_kv, piece_owner, cache_len, out_weight
):
    kvheads_local = tree_kv.shape[-1] // (2 * HD)
    heads_local = queries.shape[-1] // HD
    group_size = heads_local // kvheads_local
    tree_size = queries.shape[1]
    slot_count = cache_kv.shape[0]
    piece_rows = cache_kv.shape[1]
    depth_most = accepted_path.shape[1]
    scaling = 1.0 / math.sqrt(HD)
    every_query = lax.all_gather(queries, "req", axis=0, tiled=True)
    req_total = every_query.shape[0]
    owner_req = piece_owner[:, 0]
    owner_piece = piece_owner[:, 1]
    safe_req = jnp.maximum(owner_req, 0)
    slot_query = every_query[safe_req].reshape(slot_count, tree_size, kvheads_local, group_size, HD)
    stored = cache_kv.reshape(slot_count, piece_rows, kvheads_local, 2, HD)
    row_pos = owner_piece[:, None] * piece_rows + lax.broadcasted_iota(
        jnp.int32, (slot_count, piece_rows), 1
    )
    visible = (owner_req >= 0)[:, None] & (row_pos < cache_len[safe_req][:, None])
    wide_mask = visible[:, None, None, None, :]
    scores = (
        jnp.einsum(
            "stkgd,spkd->stkgp", slot_query, stored[:, :, :, 0], preferred_element_type=jnp.float32
        )
        * scaling
    )
    scores = jnp.where(wide_mask, scores, NEG)
    slot_peak = jnp.max(scores, -1)
    expo = jnp.where(wide_mask, jnp.exp(scores - slot_peak[..., None]), 0.0)
    slot_den = jnp.sum(expo, -1)
    weights = expo.astype(jnp.bfloat16)
    slot_num = jnp.einsum(
        "stkgp,spkd->stkgd", weights, stored[:, :, :, 1], preferred_element_type=jnp.float32
    )
    request_ids = lax.broadcasted_iota(jnp.int32, (req_total, slot_count), 0)
    member = (owner_req[None, :] == request_ids)[:, :, None, None, None]
    req_peak = jnp.max(jnp.where(member, slot_peak[None], NEG), axis=1)
    factor = jnp.where(
        member, jnp.exp(jnp.where(member, slot_peak[None] - req_peak[:, None], 0.0)), 0.0
    )
    req_den = jnp.sum(factor * slot_den[None], axis=1)
    req_num = jnp.einsum("rstkg,stkgd->rtkgd", factor, slot_num, precision=lax.Precision.HIGHEST)
    peak_table = req_peak.reshape(req_total, tree_size, heads_local)
    den_table = req_den.reshape(req_total, tree_size, heads_local)
    num_table = req_num.reshape(req_total, tree_size, heads_local * HD)
    own_index = lax.axis_index("req")
    got_peak, got_den, got_num = (
        lax.all_to_all(
            peak_table.astype(jnp.bfloat16), "req", split_axis=0, concat_axis=0, tiled=True
        ).astype(peak_table.dtype),
        lax.all_to_all(
            den_table.astype(jnp.bfloat16), "req", split_axis=0, concat_axis=0, tiled=True
        ).astype(den_table.dtype),
        lax.all_to_all(
            num_table.astype(jnp.bfloat16), "req", split_axis=0, concat_axis=0, tiled=True
        ).astype(num_table.dtype),
    )
    cache_peak = jnp.max(got_peak, axis=0)
    source_scale = jnp.exp(got_peak - cache_peak[None])
    cache_den = jnp.sum(source_scale * got_den, axis=0)
    got_rows = got_num.reshape(got_num.shape[0], tree_size, heads_local, HD)
    cache_num = jnp.sum(source_scale[..., None] * got_rows, axis=0)
    reached = ancestors(tree_parent)[0]
    home_query = queries[0].reshape(tree_size, kvheads_local, group_size, HD)
    fresh = tree_kv[0].reshape(tree_size, kvheads_local, 2, HD)
    tree_mask = reached[:, None, None, :] > 0.5
    tree_scores = (
        jnp.einsum("ikgd,jkd->ikgj", home_query, fresh[:, :, 0], preferred_element_type=jnp.float32)
        * scaling
    )
    tree_scores = jnp.where(tree_mask, tree_scores, NEG)
    tree_peak = jnp.max(tree_scores, -1)
    tree_exp = jnp.where(tree_mask, jnp.exp(tree_scores - tree_peak[..., None]), 0.0)
    tree_den = jnp.sum(tree_exp, -1).reshape(tree_size, heads_local)
    tree_num = jnp.einsum(
        "ikgj,jkd->ikgd",
        tree_exp.astype(jnp.bfloat16),
        fresh[:, :, 1],
        preferred_element_type=jnp.float32,
    )
    tree_num = tree_num.reshape(tree_size, heads_local, HD)
    tree_peak = tree_peak.reshape(tree_size, heads_local)
    total_peak = jnp.maximum(cache_peak, tree_peak)
    cache_scale = jnp.exp(cache_peak - total_peak)
    tree_scale = jnp.exp(tree_peak - total_peak)
    denom = cache_den * cache_scale + tree_den * tree_scale
    numer = cache_num * cache_scale[..., None] + tree_num * tree_scale[..., None]
    attention = (
        (numer / denom[..., None]).reshape(1, tree_size, heads_local * HD).astype(jnp.bfloat16)
    )
    piece = lax.all_gather(attention, "req", axis=0, tiled=True)
    flat_rows = piece.reshape(piece.shape[0] * piece.shape[1], piece.shape[2])
    product = jnp.dot(flat_rows, out_weight, preferred_element_type=jnp.float32)
    terms = product.reshape(piece.shape[0], piece.shape[1], out_weight.shape[1])
    mixed = lax.psum_scatter(terms.astype(jnp.bfloat16), "tp", scatter_dimension=0, tiled=True)
    own_path = lax.dynamic_index_in_dim(accepted_path, own_index, 0, keepdims=False)
    picked = tree_kv[0][jnp.maximum(own_path, 0)]
    picked = jnp.where((own_path >= 0)[:, None], picked, jnp.zeros_like(picked))
    all_rows = lax.all_gather(picked[None], "req", axis=0, tiled=True)
    counts = jnp.sum((accepted_path >= 0).astype(jnp.int32), axis=1)
    offset = row_pos - cache_len[safe_req][:, None]
    writing = (owner_req >= 0)[:, None] & (offset >= 0) & (offset < counts[safe_req][:, None])
    slot_rows = all_rows[safe_req]
    chosen = jnp.take_along_axis(slot_rows, jnp.clip(offset, 0, depth_most - 1)[:, :, None], axis=1)
    cache_out = jnp.where(writing[:, :, None], chosen, cache_kv)
    return (mixed, cache_out)


def solution(mesh):
    return jax.shard_map(
        shards,
        mesh=mesh,
        in_specs=(
            P("req", None, "tp"),
            P("req", None, "tp"),
            P("req", None),
            P(),
            P("req", None, "tp"),
            P("req", None),
            P(),
            P("tp", "req"),
        ),
        out_specs=(P("tp", None, "req"), P("req", None, "tp")),
        check_vma=False,
    )
```

profile of v0, /device:TPU:2, one launch (start us, length us, event | category | flops | bytes accessed | tf_op | source)
XLA Modules:
  0.0 331.0 jit_solution(16705288890588195445)
XLA Ops:
  7.2 0.7 all-gather.3.cloned.1.call-update
  7.9 1.2 copy.126
  9.1 0.8 slice_bitcast_fusion.4
  9.9 0.7 convert_reduce_fusion
  10.6 0.6 gather_fusion.2
  11.2 1.3 gather_fusion
  12.6 0.7 compare_bitcast_fusion
  13.3 84.3 %all-gather.3.cloned.1.call-done = bf16[64,28,512]{2,1,0:T(8,128)(2,1)} async-done(((bf16[1,28,512]{2,1,0:T(8,128)(2,1)}), bf16[64,28,512]{2,1,0:T(8,128)(2,1)}) %all-gather.3.cloned.1.call-update) | async-done | bytes 1835024 | tf_op jit(solution)/shard_map/all_gather | solution.py:34
  97.6 2.1 gather_fusion.1
  99.8 0.3 fusion.62
  100.2 0.2 fusion.11
  100.5 0.3 fusion.19
  100.7 0.2 select_reduce_fusion
  100.9 0.8 copy.130
  101.7 8.0 %all-to-all-start = ((bf16[64,28,4]{1,2,0:T(4,128)(2,1)}), bf16[64,28,4]{1,2,0:T(4,128)(2,1)S(1)}, u32[]{:S(2)}, u32[]{:S(2)}) async-start(bf16[64,28,4]{1,2,0:T(4,128)(2,1)} %copy.130), calls=%async_computation | async-start | bytes 131072 | tf_op jit(solution)/shard_map/all_to_all | solution.py:73
  109.8 0.3 multiply_reduce_fusion.1
  110.2 0.8 copy.151
  110.9 7.5 %all-to-all-done = bf16[64,28,4]{1,2,0:T(4,128)(2,1)S(1)} async-done(((bf16[64,28,4]{1,2,0:T(4,128)(2,1)}), bf16[64,28,4]{1,2,0:T(4,128)(2,1)S(1)}, u32[]{:S(2)}, u32[]{:S(2)}) %all-to-all-start) | async-done | bytes 14368 | tf_op jit(solution)/shard_map/all_to_all | solution.py:73
  118.5 5.5 %all-to-all-start.2 = ((bf16[64,28,4]{1,2,0:T(4,128)(2,1)}), bf16[64,28,4]{1,2,0:T(4,128)(2,1)S(1)}, u32[]{:S(2)}, u32[]{:S(2)}) async-start(bf16[64,28,4]{1,2,0:T(4,128)(2,1)} %copy.151), calls=%async_computation.2 | async-start | bytes 131072 | tf_op jit(solution)/shard_map/all_to_all | solution.py:76
  124.0 6.0 %convert_bitcast_fusion = bf16[64,28,1,4,128]{4,0,3,1,2:T(8,128)(2,1)S(1)} fusion(f32[3,28,4,128]{3,1,2,0:T(8,128)S(1)} %fusion.19, f32[64,28,4]{0,2,1:T(4,128)S(1)} %select_reduce_fusion, f32[3,28,4]{0,2,1:T(4,128)S(1)} %copy.137, pred[64,3]{0,1:T(4,128)(4,1)S(1)} %iota_compare_fusion), kind=kOutput, calls=%fused_computation.9 | convolution fusion | flops 34012160 | bytes 2037248 | tf_op jit(solution)/shard_map/rstkg,stkgd->rtkgd/dot_general | solution.py:67
  130.0 1.4 copy.161
  131.4 1.8 reshape.676
  133.3 10.7 %all-to-all-start.1 = ((bf16[64,28,512]{2,1,0:T(8,128)(2,1)}), bf16[64,28,512]{2,1,0:T(8,128)(2,1)S(1)}, u32[]{:S(2)}, u32[]{:S(2)}) async-start(bf16[64,28,512]{2,1,0:T(8,128)(2,1)} %reshape.676), calls=%async_computation.1 | async-start | bytes 4194304 | tf_op jit(solution)/shard_map/all_to_all | solution.py:79
  144.5 0.1 convolution_minimum_fusion.2
  144.8 0.2 fusion.10
  145.1 0.2 fusion.61
  145.3 0.2 convolution_bitcast_fusion
  146.0 0.2 subtract_exponential_fusion
  146.6 0.4 copy.135
  147.0 3.5 %mul.113 = f32[64,28,4,128]{3,2,0,1:T(4,128)} broadcast(f32[64,28,4]{2,0,1:T(8,128)S(1)} %copy.135), dimensions={0,1,2} | broadcast | bytes 3698688 | tf_op jit(solution)/shard_map/mul | solution.py:87
  150.5 5.2 %mul.114 = f32[64,28,512]{2,0,1:T(8,128)} reshape(f32[64,28,4,128]{3,2,0,1:T(4,128)} %mul.113) | data formatting | bytes 7340032 | tf_op jit(solution)/shard_map/mul | solution.py:87
  155.7 37.8 %all-to-all-done.1 = bf16[64,28,512]{2,1,0:T(8,128)(2,1)S(1)} async-done(((bf16[64,28,512]{2,1,0:T(8,128)(2,1)}), bf16[64,28,512]{2,1,0:T(8,128)(2,1)S(1)}, u32[]{:S(2)}, u32[]{:S(2)}) %all-to-all-start.1) | async-done | bytes 1835040 | tf_op jit(solution)/shard_map/all_to_all | solution.py:79
  193.5 3.6 %multiply_reduce_fusion = f32[28,512]{1,0:T(8,128)S(1)} fusion(f32[64,28,512]{2,0,1:T(8,128)} %mul.114, bf16[64,28,512]{2,1,0:T(8,128)(2,1)S(1)} %all-to-all-done.1), kind=kLoop, calls=%fused_computation.6 | loop fusion | flops 2738176 | bytes 5562368 | tf_op jit(solution)/shard_map/reduce_sum | solution.py:87
  197.5 0.6 copy.156
  198.2 0.2 maximum_reduce_fusion
  198.4 0.6 gather_fusion.3
  199.0 0.2 compare_reduce_fusion
  199.2 37.4 %all_gather.11 = bf16[64,8,256]{2,1,0:T(8,128)(2,1)S(1)} all-gather(bf16[1,8,256]{2,1,0:T(8,128)(2,1)S(1)} %bitcast_select_fusion), channel_id=1, replica_groups=mesh['req'=64,'tp'=8] {'req'}, dimensions={0}, use_global_device_ids=true | all-gather | bytes 266240 | tf_op jit(solution)/shard_map/all_gather | solution.py:124
  236.7 0.5 gather_fusion.4
  237.2 41.2 %all-gather.5.cloned.1.call-done = bf16[64,28,512]{2,1,0:T(8,128)(2,1)} async-done(((bf16[1,28,512]{2,1,0:T(8,128)(2,1)}), bf16[64,28,512]{2,1,0:T(8,128)(2,1)}) %all-gather.5.cloned.1.call-update) | async-done | bytes 1835024 | tf_op jit(solution)/shard_map/all_gather | solution.py:116
  278.4 3.7 %fusion.2 = bf16[64,28,64]{2,0,1:T(8,128)(2,1)S(1)} fusion(bf16[64,28,512]{2,1,0:T(8,128)(2,1)} %all-gather.5.cloned.1.call-done, bf16[512,64]{0,1:T(8,128)(2,1)S(1)} %copy-done), kind=kOutput, calls=%fused_computation.10 | convolution fusion | flops 117555200 | bytes 2129920 | tf_op jit(solution)/shard_map/dot_general | solution.py:118
  282.1 0.3 copy.162
  282.4 1.1 reshape.677
  283.7 4.2 %gather_fusion.5 = bf16[768,256]{1,0:T(8,128)(2,1)S(1)} fusion(bf16[3,8,256]{2,1,0:T(8,128)(2,1)S(1)} %gather_fusion.4, s32[768]{0:T(1024)S(1)} %reshape.664), kind=kCustom, calls=%fused_computation.5 | custom fusion | bytes 792576 | tf_op jit(solution)/shard_map/jit(take_along_axis)/gather | solution.py:129
  287.9 1.0 select_select_fusion
  288.9 34.0 %reduce-scatter.4.cloned.1.call-done = bf16[8,1792]{1,0:T(8,128)(2,1)} async-done(((bf16[64,1792]{1,0:T(8,128)(2,1)}), bf16[8,1792]{1,0:T(8,128)(2,1)}) %reduce-scatter.4.cloned.1.call-update) | async-done | bytes 28688
  322.9 0.9 reshape.678
  323.8 0.6 copy.163
  (53 shorter events, 2.9 us)
Async XLA Ops:
  7.2 271.3 %copy-start = (bf16[512,64]{0,1:T(8,128)(2,1)S(1)}, bf16[512,64]{0,1:T(8,128)(2,1)}, u32[]{:S(2)}) copy-start(bf16[512,64]{0,1:T(8,128)(2,1)} %param.15) | copy-start | bytes 196612
  7.2 90.4 %all-gather.3.cloned.1.call-start = ((), (), s32[]{:S(2)}) async-start(), calls=%async_computation.4 | async-start | bytes 2129920 | tf_op jit(solution)/shard_map/all_gather | solution.py:34
  101.7 16.8 %all-to-all-start = ((bf16[64,28,4]{1,2,0:T(4,128)(2,1)}), bf16[64,28,4]{1,2,0:T(4,128)(2,1)S(1)}, u32[]{:S(2)}, u32[]{:S(2)}) async-start(bf16[64,28,4]{1,2,0:T(4,128)(2,1)} %copy.130), calls=%async_computation | async-start | bytes 131072 | tf_op jit(solution)/shard_map/all_to_all | solution.py:73
  118.5 14.8 %all-to-all-start.2 = ((bf16[64,28,4]{1,2,0:T(4,128)(2,1)}), bf16[64,28,4]{1,2,0:T(4,128)(2,1)S(1)}, u32[]{:S(2)}, u32[]{:S(2)}) async-start(bf16[64,28,4]{1,2,0:T(4,128)(2,1)} %copy.151), calls=%async_computation.2 | async-start | bytes 131072 | tf_op jit(solution)/shard_map/all_to_all | solution.py:76
  133.3 10.7 %copy-start.3 = (bf16[1,28,512]{2,1,0:T(8,128)(2,1)S(1)}, bf16[1,28,512]{2,1,0:T(8,128)(2,1)}, u32[]{:S(2)}) copy-start(bf16[1,28,512]{2,1,0:T(8,128)(2,1)} %param.8) | copy-start | bytes 86020
  133.3 10.8 %copy-start.2 = (bf16[1,28,256]{2,1,0:T(8,128)(2,1)S(1)}, bf16[1,28,256]{2,1,0:T(8,128)(2,1)}, u32[]{:S(2)}) copy-start(bf16[1,28,256]{2,1,0:T(8,128)(2,1)} %param.9) | copy-start | bytes 43012
  133.3 10.8 %copy-start.5 = (s32[1,28]{1,0:T(1,128)S(1)}, s32[1,28]{1,0:T(1,128)}, u32[]{:S(2)}) copy-start(s32[1,28]{1,0:T(1,128)} %param.10) | copy-start | bytes 340
  133.3 60.2 %all-to-all-start.1 = ((bf16[64,28,512]{2,1,0:T(8,128)(2,1)}), bf16[64,28,512]{2,1,0:T(8,128)(2,1)S(1)}, u32[]{:S(2)}, u32[]{:S(2)}) async-start(bf16[64,28,512]{2,1,0:T(8,128)(2,1)} %reshape.676), calls=%async_computation.1 | async-start | bytes 4194304 | tf_op jit(solution)/shard_map/all_to_all | solution.py:79
  143.9 134.5 %all-gather.5.cloned.1.call-start = ((), (), s32[]{:S(2)}) async-start(), calls=%async_computation.5 | async-start | bytes 2129920 | tf_op jit(solution)/shard_map/all_gather | solution.py:116
  155.7 42.5 %copy-start.4 = (s32[64,8]{0,1:T(8,128)S(1)}, s32[64,8]{0,1:T(8,128)}, u32[]{:S(2)}) copy-start(s32[64,8]{0,1:T(8,128)} %param.11) | copy-start | bytes 6148
  198.1 124.8 %reduce-scatter.4.cloned.1.call-start = ((), (), s32[]{:S(2)}) async-start(), calls=%async_computation.6 | async-start | bytes 258048
  283.6 4.3 %copy-start.1 = (bf16[3,256,256]{2,1,0:T(8,128)(2,1)S(1)}, bf16[3,256,256]{2,1,0:T(8,128)(2,1)}, u32[]{:S(2)}) copy-start(bf16[3,256,256]{2,1,0:T(8,128)(2,1)} %param.12) | copy-start | bytes 1179652
Sparse Core Ops, SparseCore 0:
  11.4 86.1 all-gather.2
  198.3 80.1 all-gather.4
  283.7 39.1 reduce-scatter.3
where the time goes:
time: 332 us; the launch traced here: 331 us
  waiting for transfers between devices  206 us (62%)
  blocking collectives  37.4 us (11%)
  local copies, waits for them, and re-layouts  29.6 us (9%)
  starting transfers between devices  24.3 us (7%)
  between operations  14.1 us (4%)
  matrix products  11.4 us (3%)
  other arithmetic  8.73 us (3%)
    all_gather x1, waiting for transfers between devices, shards(): every_query = lax.all_gather(queries, 'req', axis=0, tiled=True)  84.3 us
    all_gather x1, waiting for transfers between devices, shards(): piece = lax.all_gather(attention, 'req', axis=0, tiled=True)  41.2 us
    all_to_all x1, waiting for transfers between devices, shards(): lax.all_to_all(num_table.astype(jnp.bfloat16), 'req', split_axis=0, conca...  37.8 us
    all_gather x1, blocking collectives, shards(): all_rows = lax.all_gather(picked[None], 'req', axis=0, tiled=True)  37.4 us
    unnamed x4, waiting for transfers between devices  34.7 us
    all_to_all x1, starting transfers between devices, shards(): lax.all_to_all(num_table.astype(jnp.bfloat16), 'req', split_axis=0, conca...  10.7 us
    mul x2, local copies, waits for them, and re-layouts, shards(): cache_num = jnp.sum(source_scale[..., None] * got_rows, axis=0)  8.76 us
    all_to_all x1, starting transfers between devices, shards(): lax.all_to_all(peak_table.astype(jnp.bfloat16), 'req', split_axis=0, conc...  7.97 us
  transfers between devices with their start and end apart: 6, of which 5 were waited for; matrix products, arithmetic and copies ran while one was open for 10% of the time, Pallas kernels for 0%

commit v1 on v0

--- a/solution.py
+++ b/solution.py
@@ -31,7 +31,9 @@
     piece_rows = cache_kv.shape[1]
     depth_most = accepted_path.shape[1]
     scaling = 1.0 / math.sqrt(HD)
-    every_query = lax.all_gather(queries, "req", axis=0, tiled=True)
+    every_query = jnp.concatenate(
+        lax.all_to_all(jnp.stack([queries] * lax.axis_size("req")), "req", 0, 0), axis=0
+    )
     req_total = every_query.shape[0]
     owner_req = piece_owner[:, 0]
     owner_piece = piece_owner[:, 1]

time: 332 us -> 305 us (0.919)
  waiting for transfers between devices: 206 us -> 167 us
  starting transfers between devices: 24.3 us -> 34.6 us
    all_gather x1 -> x0, waiting for transfers between devices: 84.3 us -> none  [shards(): every_query = lax.all_gather(queries, 'req', axis=0, tiled=True)]
    all_to_all x0 -> x1, waiting for transfers between devices: none -> 47.2 us  [shards(): lax.all_to_all(jnp.stack([queries] * lax.axis_size('req')), 'req', 0, 0)]
    all_to_all x0 -> x1, starting transfers between devices: none -> 10.8 us  [shards(): lax.all_to_all(jnp.stack([queries] * lax.axis_size('req')), 'req', 0, 0)]
    all_to_all x1, waiting for transfers between devices: 37.8 us -> 34.4 us  [shards(): lax.all_to_all(num_table.astype(jnp.bfloat16), 'req', split_axis=0, conca...]
    unnamed x4 -> x3, waiting for transfers between devices: 34.7 us -> 34 us
  transfers between devices with their start and end apart: 6 -> 6, of which waited for: 5 -> 5; matrix products, arithmetic and copies ran while one was open for 10% -> 11% of each run, Pallas kernels for 0% -> 0%
where the time goes in v1:
time: 305 us; the launch traced here: 304 us
  waiting for transfers between devices  167 us (55%)
  blocking collectives  37.4 us (12%)
  starting transfers between devices  34.6 us (11%)
  local copies, waits for them, and re-layouts  31.4 us (10%)
  between operations  14.5 us (5%)
  matrix products  11.3 us (4%)
  other arithmetic  7.49 us (2%)
    all_to_all x1, waiting for transfers between devices, shards(): lax.all_to_all(jnp.stack([queries] * lax.axis_size('req')), 'req', 0, 0)  47.2 us
    all_gather x1, waiting for transfers between devices, shards(): piece = lax.all_gather(attention, 'req', axis=0, tiled=True)  44.1 us
    all_gather x1, blocking collectives, shards(): all_rows = lax.all_gather(picked[None], 'req', axis=0, tiled=True)  37.4 us
    all_to_all x1, waiting for transfers between devices, shards(): lax.all_to_all(num_table.astype(jnp.bfloat16), 'req', split_axis=0, conca...  34.4 us
    unnamed x3, waiting for transfers between devices  34 us
    all_to_all x1, starting transfers between devices, shards(): lax.all_to_all(jnp.stack([queries] * lax.axis_size('req')), 'req', 0, 0)  10.8 us
    all_to_all x1, starting transfers between devices, shards(): lax.all_to_all(num_table.astype(jnp.bfloat16), 'req', split_axis=0, conca...  10.5 us
    mul x2, local copies, waits for them, and re-layouts, shards(): cache_num = jnp.sum(source_scale[..., None] * got_rows, axis=0)  8.76 us
  transfers between devices with their start and end apart: 6, of which 5 were waited for; matrix products, arithmetic and copies ran while one was open for 11% of the time, Pallas kernels for 0%

profile of v1, /device:TPU:2, one launch (start us, length us, event | category | flops | bytes accessed | tf_op | source)
XLA Modules:
  0.0 304.1 jit_solution(11283914893103346649)
XLA Ops:
  7.2 2.4 stack.2
  9.6 10.8 %all-to-all-start = ((bf16[64,1,28,512]{3,2,1,0:T(8,128)(2,1)}), bf16[64,1,28,512]{3,2,1,0:T(8,128)(2,1)S(1)}, u32[]{:S(2)}, u32[]{:S(2)}) async-start(bf16[64,1,28,512]{3,2,1,0:T(8,128)(2,1)} %stack.2), calls=%async_computation | async-start | bytes 4194304 | tf_op jit(solution)/shard_map/all_to_all | solution.py:35
  20.7 0.6 gather_fusion.2
  21.3 0.6 gather_fusion
  22.0 0.7 fusion.50
  22.7 47.2 %all-to-all-done = bf16[64,1,28,512]{3,2,1,0:T(8,128)(2,1)S(1)} async-done(((bf16[64,1,28,512]{3,2,1,0:T(8,128)(2,1)}), bf16[64,1,28,512]{3,2,1,0:T(8,128)(2,1)S(1)}, u32[]{:S(2)}, u32[]{:S(2)}) %all-to-all-start) | async-done | bytes 1835040 | tf_op jit(solution)/shard_map/all_to_all | solution.py:35
  69.9 0.6 gather_fusion.1
  70.5 0.3 fusion.62
  70.9 0.2 fusion.11
  71.2 0.2 fusion.19
  71.4 0.2 select_reduce_fusion
  71.7 0.8 copy.129
  72.4 7.5 %all-to-all-start.1 = ((bf16[64,28,4]{1,2,0:T(4,128)(2,1)}), bf16[64,28,4]{1,2,0:T(4,128)(2,1)S(1)}, u32[]{:S(2)}, u32[]{:S(2)}) async-start(bf16[64,28,4]{1,2,0:T(4,128)(2,1)} %copy.129), calls=%async_computation.1 | async-start | bytes 131072 | tf_op jit(solution)/shard_map/all_to_all | solution.py:75
  80.1 0.3 multiply_reduce_fusion.1
  80.5 0.8 copy.150
  81.2 7.5 %all-to-all-done.1 = bf16[64,28,4]{1,2,0:T(4,128)(2,1)S(1)} async-done(((bf16[64,28,4]{1,2,0:T(4,128)(2,1)}), bf16[64,28,4]{1,2,0:T(4,128)(2,1)S(1)}, u32[]{:S(2)}, u32[]{:S(2)}) %all-to-all-start.1) | async-done | bytes 14368 | tf_op jit(solution)/shard_map/all_to_all | solution.py:75
  88.8 5.5 %all-to-all-start.3 = ((bf16[64,28,4]{1,2,0:T(4,128)(2,1)}), bf16[64,28,4]{1,2,0:T(4,128)(2,1)S(1)}, u32[]{:S(2)}, u32[]{:S(2)}) async-start(bf16[64,28,4]{1,2,0:T(4,128)(2,1)} %copy.150), calls=%async_computation.3 | async-start | bytes 131072 | tf_op jit(solution)/shard_map/all_to_all | solution.py:78
  94.3 6.0 %convert_bitcast_fusion = bf16[64,28,1,4,128]{4,0,3,1,2:T(8,128)(2,1)S(1)} fusion(f32[3,28,4,128]{3,1,2,0:T(8,128)S(1)} %fusion.19, f32[64,28,4]{0,2,1:T(4,128)S(1)} %select_reduce_fusion, f32[3,28,4]{0,2,1:T(4,128)S(1)} %copy.136, pred[64,3]{0,1:T(4,128)(4,1)S(1)} %iota_compare_fusion), kind=kOutput, calls=%fused_computation.9 | convolution fusion | flops 34012160 | bytes 2037248 | tf_op jit(solution)/shard_map/rstkg,stkgd->rtkgd/dot_general | solution.py:69
  100.3 1.4 copy.160
  101.7 1.8 reshape.683
  103.6 10.5 %all-to-all-start.2 = ((bf16[64,28,512]{2,1,0:T(8,128)(2,1)}), bf16[64,28,512]{2,1,0:T(8,128)(2,1)S(1)}, u32[]{:S(2)}, u32[]{:S(2)}) async-start(bf16[64,28,512]{2,1,0:T(8,128)(2,1)} %reshape.683), calls=%async_computation.2 | async-start | bytes 4194304 | tf_op jit(solution)/shard_map/all_to_all | solution.py:81
  114.1 0.3 all-gather.2.cloned.1.call-start
  115.4 0.2 fusion.61
  115.6 0.2 convolution_bitcast_fusion
  116.3 0.7 subtract_exponential_fusion
  117.2 0.7 copy.154
  117.9 0.7 copy.148
  118.6 0.7 copy.144
  119.2 1.2 copy.134
  120.4 3.5 %mul.113 = f32[64,28,4,128]{3,2,0,1:T(4,128)} broadcast(f32[64,28,4]{2,0,1:T(8,128)S(1)} %copy.134), dimensions={0,1,2} | broadcast | bytes 3698688 | tf_op jit(solution)/shard_map/mul | solution.py:89
  124.0 5.2 %mul.114 = f32[64,28,512]{2,0,1:T(8,128)} reshape(f32[64,28,4,128]{3,2,0,1:T(4,128)} %mul.113) | data formatting | bytes 7340032 | tf_op jit(solution)/shard_map/mul | solution.py:89
  129.2 34.4 %all-to-all-done.2 = bf16[64,28,512]{2,1,0:T(8,128)(2,1)S(1)} async-done(((bf16[64,28,512]{2,1,0:T(8,128)(2,1)}), bf16[64,28,512]{2,1,0:T(8,128)(2,1)S(1)}, u32[]{:S(2)}, u32[]{:S(2)}) %all-to-all-start.2) | async-done | bytes 1835040 | tf_op jit(solution)/shard_map/all_to_all | solution.py:81
  163.6 3.3 %multiply_reduce_fusion = f32[28,512]{1,0:T(8,128)S(1)} fusion(f32[64,28,512]{2,0,1:T(8,128)} %mul.114, bf16[64,28,512]{2,1,0:T(8,128)(2,1)S(1)} %all-to-all-done.2), kind=kLoop, calls=%fused_computation.6 | loop fusion | flops 2738176 | bytes 5562368 | tf_op jit(solution)/shard_map/reduce_sum | solution.py:89
  167.4 0.6 copy.155
  168.1 0.2 maximum_reduce_fusion
  168.3 0.6 gather_fusion.3
  168.8 0.2 compare_reduce_fusion
  169.1 37.4 %all_gather.7 = bf16[64,8,256]{2,1,0:T(8,128)(2,1)S(1)} all-gather(bf16[1,8,256]{2,1,0:T(8,128)(2,1)S(1)} %bitcast_select_fusion), channel_id=1, replica_groups=mesh['req'=64,'tp'=8] {'req'}, dimensions={0}, use_global_device_ids=true | all-gather | bytes 266240 | tf_op jit(solution)/shard_map/all_gather | solution.py:126
  206.6 0.5 gather_fusion.4
  207.1 44.1 %all-gather.2.cloned.1.call-done = bf16[64,28,512]{2,1,0:T(8,128)(2,1)} async-done(((bf16[1,28,512]{2,1,0:T(8,128)(2,1)}), bf16[64,28,512]{2,1,0:T(8,128)(2,1)}) %all-gather.2.cloned.1.call-update) | async-done | bytes 1835024 | tf_op jit(solution)/shard_map/all_gather | solution.py:118
  251.2 3.7 %fusion.2 = bf16[64,28,64]{2,0,1:T(8,128)(2,1)S(1)} fusion(bf16[64,28,512]{2,1,0:T(8,128)(2,1)} %all-gather.2.cloned.1.call-done, bf16[512,64]{0,1:T(8,128)(2,1)S(1)} %copy-done), kind=kOutput, calls=%fused_computation.10 | convolution fusion | flops 117555200 | bytes 2129920 | tf_op jit(solution)/shard_map/dot_general | solution.py:120
  255.0 0.3 copy.161
  255.3 1.1 reshape.684
  256.5 4.2 %gather_fusion.5 = bf16[768,256]{1,0:T(8,128)(2,1)S(1)} fusion(bf16[3,8,256]{2,1,0:T(8,128)(2,1)S(1)} %gather_fusion.4, s32[768]{0:T(1024)S(1)} %reshape.671), kind=kCustom, calls=%fused_computation.5 | custom fusion | bytes 792576 | tf_op jit(solution)/shard_map/jit(take_along_axis)/gather | solution.py:131
  260.7 1.0 select_select_fusion
  261.8 34.0 %reduce-scatter.4.cloned.1.call-done = bf16[8,1792]{1,0:T(8,128)(2,1)} async-done(((bf16[64,1792]{1,0:T(8,128)(2,1)}), bf16[8,1792]{1,0:T(8,128)(2,1)}) %reduce-scatter.4.cloned.1.call-update) | async-done | bytes 28688
  295.7 0.9 reshape.685
  296.6 0.6 copy.162
  (75 shorter events, 3.0 us)
Async XLA Ops:
  7.2 244.1 %copy-start = (bf16[512,64]{0,1:T(8,128)(2,1)S(1)}, bf16[512,64]{0,1:T(8,128)(2,1)}, u32[]{:S(2)}) copy-start(bf16[512,64]{0,1:T(8,128)(2,1)} %param.15) | copy-start | bytes 196612
  9.6 10.8 %copy-start.2 = (bf16[3,256,256]{2,1,0:T(8,128)(2,1)S(1)}, bf16[3,256,256]{2,1,0:T(8,128)(2,1)}, u32[]{:S(2)}) copy-start(bf16[3,256,256]{2,1,0:T(8,128)(2,1)} %param.12) | copy-start | bytes 1179652
  9.6 11.0 %copy-start.15 = (s32[3,2]{0,1:T(2,128)S(1)}, s32[3,2]{0,1:T(2,128)}, u32[]{:S(2)}) copy-start(s32[3,2]{0,1:T(2,128)} %param.13) | copy-start | bytes 76
  9.6 11.1 %copy-start.8 = (s32[64,8]{0,1:T(8,128)S(1)}, s32[64,8]{0,1:T(8,128)}, u32[]{:S(2)}) copy-start(s32[64,8]{0,1:T(8,128)} %param.11) | copy-start | bytes 6148
  9.6 11.7 %copy-start.1 = (s32[64]{0:T(128)S(1)}, s32[64]{0:T(128)}, u32[]{:S(2)}) copy-start(s32[64]{0:T(128)} %param.14) | copy-start | bytes 772
  9.6 60.3 %all-to-all-start = ((bf16[64,1,28,512]{3,2,1,0:T(8,128)(2,1)}), bf16[64,1,28,512]{3,2,1,0:T(8,128)(2,1)S(1)}, u32[]{:S(2)}, u32[]{:S(2)}) async-start(bf16[64,1,28,512]{3,2,1,0:T(8,128)(2,1)} %stack.2), calls=%async_computation | async-start | bytes 4194304 | tf_op jit(solution)/shard_map/all_to_all | solution.py:35
  20.6 50.3 %copy-start.9 = (s32[3]{0:T(128)}, s32[3]{0:T(128)S(1)}, u32[]{:S(2)}) copy-start(s32[3]{0:T(128)S(1)} %get-tuple-element.14) | copy-start | bytes 40
  21.9 48.6 %copy-start.11 = (s32[3]{0:T(128)}, s32[3]{0:T(128)S(1)}, u32[]{:S(2)}) copy-start(s32[3]{0:T(128)S(1)} %gather_fusion) | copy-start | bytes 40
  72.4 16.4 %all-to-all-start.1 = ((bf16[64,28,4]{1,2,0:T(4,128)(2,1)}), bf16[64,28,4]{1,2,0:T(4,128)(2,1)S(1)}, u32[]{:S(2)}, u32[]{:S(2)}) async-start(bf16[64,28,4]{1,2,0:T(4,128)(2,1)} %copy.129), calls=%async_computation.1 | async-start | bytes 131072 | tf_op jit(solution)/shard_map/all_to_all | solution.py:75
  88.8 14.8 %all-to-all-start.3 = ((bf16[64,28,4]{1,2,0:T(4,128)(2,1)}), bf16[64,28,4]{1,2,0:T(4,128)(2,1)S(1)}, u32[]{:S(2)}, u32[]{:S(2)}) async-start(bf16[64,28,4]{1,2,0:T(4,128)(2,1)} %copy.150), calls=%async_computation.3 | async-start | bytes 131072 | tf_op jit(solution)/shard_map/all_to_all | solution.py:78
  103.6 10.8 %copy-start.4 = (bf16[1,28,512]{2,1,0:T(8,128)(2,1)S(1)}, bf16[1,28,512]{2,1,0:T(8,128)(2,1)}, u32[]{:S(2)}) copy-start(bf16[1,28,512]{2,1,0:T(8,128)(2,1)} %param.8) | copy-start | bytes 86020
  103.6 10.8 %copy-start.3 = (bf16[1,28,256]{2,1,0:T(8,128)(2,1)S(1)}, bf16[1,28,256]{2,1,0:T(8,128)(2,1)}, u32[]{:S(2)}) copy-start(bf16[1,28,256]{2,1,0:T(8,128)(2,1)} %param.9) | copy-start | bytes 43012
  103.6 10.8 %copy-start.16 = (s32[1,28]{1,0:T(1,128)S(1)}, s32[1,28]{1,0:T(1,128)}, u32[]{:S(2)}) copy-start(s32[1,28]{1,0:T(1,128)} %param.10) | copy-start | bytes 340
  103.6 60.0 %all-to-all-start.2 = ((bf16[64,28,512]{2,1,0:T(8,128)(2,1)}), bf16[64,28,512]{2,1,0:T(8,128)(2,1)S(1)}, u32[]{:S(2)}, u32[]{:S(2)}) async-start(bf16[64,28,512]{2,1,0:T(8,128)(2,1)} %reshape.683), calls=%async_computation.2 | async-start | bytes 4194304 | tf_op jit(solution)/shard_map/all_to_all | solution.py:81
  114.1 137.2 %all-gather.2.cloned.1.call-start = ((), (), s32[]{:S(2)}) async-start(), calls=%async_computation.5 | async-start | bytes 2129920 | tf_op jit(solution)/shard_map/all_gather | solution.py:118
  129.2 37.7 %copy-start.5 = (f32[28,4]{1,0:T(8,128)S(1)}, f32[28,4]{1,0:T(8,128)}, u32[]{:S(2)}) copy-start(f32[28,4]{1,0:T(8,128)} %copy.154) | copy-start | bytes 1348
  129.2 37.8 %copy-start.6 = (f32[28,4]{1,0:T(8,128)S(1)}, f32[28,4]{1,0:T(8,128)}, u32[]{:S(2)}) copy-start(f32[28,4]{1,0:T(8,128)} %copy.148) | copy-start | bytes 1348
  129.2 37.9 %copy-start.7 = (f32[28,4]{1,0:T(8,128)S(1)}, f32[28,4]{1,0:T(8,128)}, u32[]{:S(2)}) copy-start(f32[28,4]{1,0:T(8,128)} %copy.144) | copy-start | bytes 1348
  168.0 127.7 %reduce-scatter.4.cloned.1.call-start = ((), (), s32[]{:S(2)}) async-start(), calls=%async_computation.6 | async-start | bytes 258048
  207.1 49.3 %copy-start.10 = (s32[3]{0:T(128)S(1)}, s32[3]{0:T(128)}, u32[]{:S(2)}) copy-start(s32[3]{0:T(128)} %copy-done.9) | copy-start | bytes 40
  207.1 49.3 %copy-start.12 = (s32[3]{0:T(128)S(1)}, s32[3]{0:T(128)}, u32[]{:S(2)}) copy-start(s32[3]{0:T(128)} %copy-done.11) | copy-start | bytes 40
  256.4 4.3 %copy-start.13 = (pred[3,256]{1,0:T(4,128)(4,1)S(1)}, pred[3,256]{1,0:T(4,128)(4,1)}, u32[]{:S(2)}) copy-start(pred[3,256]{1,0:T(4,128)(4,1)} %get-tuple-element.9) | copy-start | bytes 2308
  256.4 4.4 %copy-start.14 = (pred[3,256]{1,0:T(4,128)(4,1)S(1)}, pred[3,256]{1,0:T(4,128)(4,1)}, u32[]{:S(2)}) copy-start(pred[3,256]{1,0:T(4,128)(4,1)} %get-tuple-element.11) | copy-start | bytes 2308
Sparse Core Ops, SparseCore 0:
  168.1 83.0 all-gather.1
  256.5 39.1 reduce-scatter.3
